TPU v7x, 32 devices: a whole 2x2x4 slice. The times are simulated.
32 devices in a mesh: sector: 8 (over y, x, core), slab: 4 (over z).
Axes of the slice: x: 2, y: 2, z: 4, core: 2. Of those that a mesh axis runs over, the one named last changes fastest.
Arguments:
- iterate: float32 [32, 60, 4096], P('slab', None, 'sector'), may hold values from -6 to 6
- right_side: float32 [32, 60, 4096], P('slab', None, 'sector'), may hold values from -6 to 6
- geometry: float32 [32, 3, 4096], P('slab', None, 'sector'), may hold values from 0.5 to 2
- temporal_block_scale: float32 [32, 4096], P('slab', 'sector'), may hold values from 1 to 2.1
- decay_rates: float32 [60], replicated, may hold values from 0.49 to 0.996
- neighbour_index: int32 [5, 4096], P(None, 'sector'), may hold values from 0 to 511, as said below
- neighbour_side: int32 [5, 4096], P(None, 'sector'), may hold values from -1 to 1, as said below
- orientation: int32 [5, 4096], P(None, 'sector'), may hold values from 0 to 2
- sector_counts: int32 [8], P('sector'), may hold values from 384 to 512, as said below
- volume_ops: float32 [4, 60, 60], replicated, may hold values from -0.75 to 0.75
- face_ops: float32 [5, 60, 180], replicated, may hold values from -0.75 to 0.75
- time_coupling: float32 [60, 60], replicated, may hold values from -0.75 to 0.75
- precondition: float32 [60, 60], replicated, may hold values from -0.375 to 0.375
Outputs:
- smoothed: float32 [32, 60, 4096], P('slab', None, 'sector')
- final_section_residual: float32 [32, 60, 4096], P('slab', None, 'sector')
Inputs may be any that keep to these rules, and one draw needn't show every extreme that they name: `sector_counts`: each sector holds from 384 to 512 live elements; some sector is full and some holds exactly 384. `neighbour_index`: faces of live elements name live elements; the first face of a slot below 192 names a slot of 320 or more, of the preceding sector or of its own; the first face of a slot from 320 up names a slot below 192, of the following sector or of its own; all other faces stay in the sector. `neighbour_side`: only the first face of a slot below 192 or from 320 up may leave the sector.
All inputs are finite; a program needn't handle non-finite values.
Results may differ from a plain program's by a relative error of at most 0.0042.
Values may be sent and summed in bfloat16 or wider, within the bound.
A program may use at most 64 MiB of HBM per device.

v0:
```python
import jax
import jax.numpy as jnp
from jax import lax
from jax.sharding import PartitionSpec as P

SECTIONS = 2


RELAX = 0.8
HIGH = lax.Precision.HIGHEST


def shifted(block, axis, distance):
    devices = range(lax.axis_size(axis))
    route = [((i - distance) % len(devices), i) for i in devices]
    return lax.ppermute(block, axis, route)


def padded(cells, sides, width):
    for axis, dim in sides:
        count = lax.axis_size(axis)
        head = lax.slice_in_dim(cells, 0, width, axis=dim)
        tail = lax.slice_in_dim(cells, cells.shape[dim] - width, cells.shape[dim], axis=dim)
        cells = jnp.concatenate(
            [
                lax.ppermute(tail, axis, [(i, (i + 1) % count) for i in range(count)]),
                cells,
                lax.ppermute(head, axis, [((i + 1) % count, i) for i in range(count)]),
            ],
            axis=dim,
        )
    return cells


def entering_2(value, axis, join, neutral):
    count, mine = (lax.axis_size(axis), lax.axis_index(axis))
    pieces = lax.all_gather(value, axis)
    so_far = jnp.full_like(value, 0) + jnp.asarray(neutral, value.dtype)

    def hop(position, so_far):
        longer = join(so_far, pieces[position])
        return jnp.where(position < mine, longer, so_far)

    return lax.fori_loop(0, count - 1, hop, so_far)


def broadcast(value, axis, source):
    kept = jnp.where(lax.axis_index(axis) == source, value, 0).astype(value.dtype)
    return lax.psum(kept, axis)


def operate(field, geometry, place, masks, volume_ops, face_ops, time_coupling, width):
    last_slab = shifted(field[-1], "slab", 1)
    previous = jnp.concatenate([last_slab[None], field[:-1]], axis=0)
    terms = jnp.einsum("dij,sje->sdie", volume_ops, field, precision=HIGH)
    applied = terms[:, 0] + jnp.sum(geometry[:, :, None, :] * terms[:, 1:], axis=1)
    extended = padded(field, (("sector", 2),), width)
    for face_id in range(face_ops.shape[0]):
        picked = jnp.take(extended, place[face_id], axis=2)
        stacked = jnp.concatenate(
            [picked * masks[face_id, rotation][None, None, :] for rotation in range(3)], axis=1
        )
        applied = applied + jnp.einsum("ij,sje->sie", face_ops[face_id], stacked, precision=HIGH)
    return applied - jnp.einsum("ij,sje->sie", time_coupling, previous, precision=HIGH)


def multiply_join(earlier, later):
    return earlier * later


def adding_join(earlier, later):
    return earlier + later


def gain_setup(scale, rate):
    factor = rate[None] / scale[:, None, :]
    own_gain = jnp.prod(factor, axis=0)
    unity = jnp.ones_like(own_gain)
    before_gain = entering_2(own_gain, "slab", multiply_join, unity)
    through_gain = before_gain * own_gain
    total_gain = broadcast(through_gain, "slab", lax.axis_size("slab") - 1)
    return (factor, before_gain, through_gain, total_gain)


def periodic_scan(source, scale, gains):
    factor, before_gain, through_gain, total_gain = gains
    values = lax.optimization_barrier(source).astype(jnp.float32)
    offset = values / scale[:, None, :]

    def compose(state, items):
        step_gain, step_offset = items
        return (step_gain * state + step_offset, None)

    nothing = jnp.zeros_like(values[0])
    own_offset, _ = lax.scan(compose, nothing, (factor, offset))
    scaled = own_offset / through_gain
    earlier = entering_2(scaled, "slab", adding_join, nothing)
    everything = lax.psum(scaled, "slab")
    before_offset = before_gain * earlier
    total_offset = total_gain * everything
    closing = total_offset / (1.0 - total_gain)
    entering = before_gain * closing + before_offset

    def advance(state, items):
        step_gain, step_offset = items
        state = step_gain * state + step_offset
        return (state, state)

    _, solved = lax.scan(advance, entering, (factor, offset))
    return solved


def on_device(
    iterate,
    right_side,
    geometry,
    temporal_block_scale,
    decay_rates,
    neighbour_index,
    neighbour_side,
    orientation,
    sector_counts,
    volume_ops,
    face_ops,
    time_coupling,
    precondition,
):
    count = iterate.shape[2]
    width = 3 * count // 8
    slots = jnp.arange(count, dtype=jnp.int32)
    live = ((slots < sector_counts[0] - width) | (slots >= count - width)).astype(jnp.float32)
    place = jnp.where(
        neighbour_side == 0,
        width + neighbour_index,
        jnp.where(
            neighbour_side < 0, neighbour_index - (count - width), count + width + neighbour_index
        ),
    )
    masks = jnp.stack(
        [(orientation == rotation).astype(jnp.float32) for rotation in range(3)], axis=1
    )
    rate = decay_rates[:, None]
    gains = gain_setup(temporal_block_scale, rate)
    field = iterate
    residual = right_side
    for section_id in range(SECTIONS):
        applied = operate(field, geometry, place, masks, volume_ops, face_ops, time_coupling, width)
        residual = live[None, None, :] * (right_side - applied)
        source = jnp.einsum("ij,sje->sie", precondition, residual, precision=HIGH).astype(
            jnp.bfloat16
        )
        correction = periodic_scan(source, temporal_block_scale, gains).astype(jnp.bfloat16)
        field = field + RELAX * correction.astype(jnp.float32)
    return (field, residual)


def solution(mesh):
    in_specs = (
        P("slab", None, "sector"),
        P("slab", None, "sector"),
        P("slab", None, "sector"),
        P("slab", "sector"),
        P(),
        P(None, "sector"),
        P(None, "sector"),
        P(None, "sector"),
        P("sector"),
        P(),
        P(),
        P(),
        P(),
    )
    out_specs = (P("slab", None, "sector"), P("slab", None, "sector"))
    return jax.shard_map(
        on_device, mesh=mesh, in_specs=in_specs, out_specs=out_specs, check_vma=False
    )
```

profile of v0, /device:TPU:0, one launch (start us, length us, event | category | flops | bytes accessed | tf_op | source)
XLA Modules:
  0.0 390.7 jit_solution(17648043873069906003)
XLA Ops:
  22.6 5.2 %convolution_bitcast_fusion.1 = f32[8,4,60,512]{3,2,1,0:T(8,128)} fusion(f32[8,60,512,1]{2,0,1,3:T(8,128)S(1)} %bitcast.258, f32[4,60,60]{2,0,1:T(4,128)S(1)} %copy-done.34), kind=kOutput, calls=%fused_computation.88 | convolution fusion | flops 707788800 | bytes 4972800 | tf_op jit(solution)/shard_map/dij,sje->sdie/dot_general | solution.py:55
  34.3 4.4 %copy.60 = f32[8,60,896]{1,0,2:T(8,128)} copy(f32[8,60,896]{2,0,1:T(8,128)} %pad_maximum_fusion.1) | data formatting | bytes 3440640 | tf_op jit(solution)/shard_map/concatenate | solution.py:24
  38.8 4.3 %gather_fusion = f32[512,8,60]{2,1,0:T(8,128)} fusion(f32[8,60,896]{1,0,2:T(8,128)} %copy.60, s32[1024]{0:T(1024)S(1)} %pad_clamp_fusion.4), kind=kCustom, calls=%fused_computation.clone | custom fusion | bytes 1968128 | tf_op jit(solution)/shard_map/jit(_take)/gather | solution.py:59
  46.3 4.3 %gather_fusion.1 = f32[512,8,60]{2,1,0:T(8,128)} fusion(f32[8,60,896]{1,0,2:T(8,128)} %copy.60, s32[1024]{0:T(1024)S(1)} %pad_clamp_fusion.3), kind=kCustom, calls=%fused_computation.1.clone | custom fusion | bytes 1968128 | tf_op jit(solution)/shard_map/jit(_take)/gather | solution.py:59
  53.9 4.3 %gather_fusion.2 = f32[512,8,60]{2,1,0:T(8,128)} fusion(f32[8,60,896]{1,0,2:T(8,128)} %copy.60, s32[1024]{0:T(1024)S(1)} %pad_clamp_fusion.2), kind=kCustom, calls=%fused_computation.2.clone | custom fusion | bytes 1968128 | tf_op jit(solution)/shard_map/jit(_take)/gather | solution.py:59
  61.4 4.3 %gather_fusion.3 = f32[512,8,60]{2,1,0:T(8,128)} fusion(f32[8,60,896]{1,0,2:T(8,128)} %copy.60, s32[1024]{0:T(1024)S(1)} %pad_clamp_fusion.1), kind=kCustom, calls=%fused_computation.3.clone | custom fusion | bytes 1968128 | tf_op jit(solution)/shard_map/jit(_take)/gather | solution.py:59
  67.9 4.3 %gather_fusion.4 = f32[512,8,60]{2,1,0:T(8,128)} fusion(f32[8,60,896]{1,0,2:T(8,128)} %copy.60, s32[1024]{0:T(1024)S(1)} %pad_clamp_fusion), kind=kCustom, calls=%fused_computation.4.clone | custom fusion | bytes 1968128 | tf_op jit(solution)/shard_map/jit(_take)/gather | solution.py:59
  76.3 4.6 %fusion.119 = f32[8,60,512]{2,1,0:T(8,128)S(1)} fusion(f32[8,60,512]{2,1,0:T(8,128)S(1)} %get-tuple-element.522, f32[8,60,512]{2,1,0:T(8,128)S(1)} %get-tuple-element.523, f32[8,60,512]{2,1,0:T(8,128)S(1)} %get-tuple-element.521, f32[8,60,512]{2,1,0:T(8,128)S(1)} %copy-done.24, f32[8,4,60,512]{3,2,1,0:T(8,128)} %convolution_bitcast_fusion.1, ...), kind=kOutput, calls=%fused_computation.110 | convolution fusion | flops 532807680 | bytes 6225920 | tf_op jit(solution)/shard_map/ij,sje->sie/dot_general | solution.py:63
  101.6 16.8 %all-gather.3 = f32[4,60,512]{2,1,0:T(8,128)} all-gather(f32[1,60,512]{2,1,0:T(8,128)S(1)} %bitcast.259), channel_id=2, replica_groups=mesh['sector'=8,'slab'=4] {'slab'}, dimensions={0}, use_global_device_ids=true | all-gather | bytes 614400 | tf_op jit(solution)/shard_map/all_gather | solution.py:37
  121.3 11.9 %while.91 = (s32[]{:T(128)}, f32[60,512]{1,0:T(8,128)}, f32[8,60,512]{2,1,0:T(8,128)S(1)}, f32[8,60,512]{2,1,0:T(8,128)S(1)}, s32[]{:T(128)}, /*index=5*/s32[]{:T(128)}) while((s32[]{:T(128)}, f32[60,512]{1,0:T(8,128)}, f32[8,60,512]{2,1,0:T(8,128)S(1)}, f32[8,60,512]{2,1,0:T(8,128)S(1)}, s32[]{:T(128)}, ...), condition=%wide.region_6.8_spmd.clone, body=%wide.region_5.7_spmd.clone.sunk | while | flops 92163 | bytes 491603 | solution.py:95
  137.0 15.4 %all-gather.4 = f32[4,60,512]{2,1,0:T(8,128)} all-gather(f32[1,60,512]{2,1,0:T(8,128)S(1)} %bitcast.260), channel_id=3, replica_groups=mesh['sector'=8,'slab'=4] {'slab'}, dimensions={0}, use_global_device_ids=true | all-gather | bytes 614400 | tf_op jit(solution)/shard_map/all_gather | solution.py:37
  156.1 35.0 %all-reduce.6.cloned.1.call-done = (f32[60,512]{1,0:T(8,128)}, f32[60,512]{1,0:T(8,128)}) async-done(((f32[60,512]{1,0:T(8,128)}, f32[60,512]{1,0:T(8,128)}), (f32[60,512]{1,0:T(8,128)}, f32[60,512]{1,0:T(8,128)})) %all-reduce.6.cloned.1.call-update) | async-done | bytes 245776 | tf_op jit(solution)/shard_map/psum | solution.py:49
  193.6 12.8 %while.88 = (s32[]{:T(128)}, f32[60,512]{1,0:T(8,128)}, bf16[8,60,512]{2,1,0:T(8,128)(2,1)}, f32[8,60,512]{2,1,0:T(8,128)S(1)}, f32[8,60,512]{2,1,0:T(8,128)S(1)}, /*index=5*/s32[]{:T(128)}) while((s32[]{:T(128)}, f32[60,512]{1,0:T(8,128)}, bf16[8,60,512]{2,1,0:T(8,128)(2,1)}, f32[8,60,512]{2,1,0:T(8,128)S(1)}, ...), condition=%wide.region_11.13_spmd, body=%wide.region_10.12_spmd.sunk | while | flops 61442 | bytes 639557 | solution.py:109
  218.2 7.8 %collective-permute-done.3 = f32[8,60,192]{2,1,0:T(8,128)S(1)} collective-permute-done((f32[8,60,192]{2,1,0:T(8,128)S(1)}, f32[8,60,192]{2,1,0:T(8,128)S(1)}, u32[]{:S(2)}, u32[]{:S(2)}) %collective-permute-start.3) | collective-permute-done | bytes 368672 | tf_op jit(solution)/shard_map/ppermute | solution.py:26
  231.9 4.3 %gather_fusion.5 = f32[512,8,60]{2,1,0:T(8,128)} fusion(f32[8,60,896]{1,0,2:T(8,128)} %copy.75, s32[1024]{0:T(1024)S(1)} %copy-done.70), kind=kCustom, calls=%fused_computation.5.clone | custom fusion | bytes 1968128 | tf_op jit(solution)/shard_map/jit(_take)/gather | solution.py:59
  236.2 4.4 %gather_fusion.6 = f32[512,8,60]{2,1,0:T(8,128)} fusion(f32[8,60,896]{1,0,2:T(8,128)} %copy.75, s32[1024]{0:T(1024)S(1)} %copy-done.72), kind=kCustom, calls=%fused_computation.6.clone | custom fusion | bytes 1968128 | tf_op jit(solution)/shard_map/jit(_take)/gather | solution.py:59
  240.6 4.4 %gather_fusion.7 = f32[512,8,60]{2,1,0:T(8,128)} fusion(f32[8,60,896]{1,0,2:T(8,128)} %copy.75, s32[1024]{0:T(1024)S(1)} %copy-done.74), kind=kCustom, calls=%fused_computation.7.clone | custom fusion | bytes 1968128 | tf_op jit(solution)/shard_map/jit(_take)/gather | solution.py:59
  244.9 4.4 %gather_fusion.8 = f32[512,8,60]{2,1,0:T(8,128)} fusion(f32[8,60,896]{1,0,2:T(8,128)} %copy.75, s32[1024]{0:T(1024)S(1)} %copy-done.76), kind=kCustom, calls=%fused_computation.8.clone | custom fusion | bytes 1968128 | tf_op jit(solution)/shard_map/jit(_take)/gather | solution.py:59
  249.4 4.3 %gather_fusion.9 = f32[512,8,60]{2,1,0:T(8,128)} fusion(f32[8,60,896]{1,0,2:T(8,128)} %copy.75, s32[1024]{0:T(1024)S(1)} %copy-done.78), kind=kCustom, calls=%fused_computation.9.clone | custom fusion | bytes 1968128 | tf_op jit(solution)/shard_map/jit(_take)/gather | solution.py:59
  284.7 4.7 %fusion.89 = f32[8,60,512]{2,1,0:T(8,128)S(1)} fusion(f32[8,60,512]{2,1,0:T(8,128)S(1)} %copy-done.9, f32[8,60,512]{2,1,0:T(8,128)S(1)} %copy-done.10, f32[8,60,512]{2,1,0:T(8,128)S(1)} %get-tuple-element.506, f32[8,60,512]{2,1,0:T(8,128)S(1)} %copy-done.14, f32[8,4,60,512]{3,2,1,0:T(8,128)} %copy-done.4, f32[5,60,180]{2,1,0:T(8,128)S(1)} %copy-done.26), kind=kOutput, calls=%fused_computation.100 | convolution fusion | flops 532807680 | bytes 6225920 | tf_op jit(solution)/shard_map/ij,sje->sie/dot_general | solution.py:63
  310.1 8.0 %while.93 = (s32[]{:T(128)}, f32[60,512]{1,0:T(8,128)S(1)}, f32[8,60,512]{2,1,0:T(8,128)S(1)}, f32[8,60,512]{2,1,0:T(8,128)}, s32[]{:T(128)}, /*index=5*/s32[]{:T(128)}) while((s32[]{:T(128)}, f32[60,512]{1,0:T(8,128)S(1)}, f32[8,60,512]{2,1,0:T(8,128)S(1)}, f32[8,60,512]{2,1,0:T(8,128)}, s32[]{:T(128)}, ...), condition=%wide.region_14.16_spmd.clone, body=%wide.region_13.15_spmd.clone.sunk | while | flops 92163 | bytes 491603 | solution.py:95
  318.2 16.2 %all-gather.5 = f32[4,60,512]{2,1,0:T(8,128)S(1)} all-gather(f32[1,60,512]{2,1,0:T(8,128)S(1)} %bitcast.261), channel_id=4, replica_groups=mesh['sector'=8,'slab'=4] {'slab'}, dimensions={0}, use_global_device_ids=true | all-gather | bytes 614400 | tf_op jit(solution)/shard_map/all_gather | solution.py:37
  338.2 34.2 %all-reduce.4.cloned.1.call-done = f32[60,512]{1,0:T(8,128)} async-done(((f32[60,512]{1,0:T(8,128)}), f32[60,512]{1,0:T(8,128)}) %all-reduce.4.cloned.1.call-update) | async-done | bytes 122896 | tf_op jit(solution)/shard_map/psum | solution.py:98
  373.4 8.2 %while.89 = (s32[]{:T(128)}, f32[60,512]{1,0:T(8,128)S(1)}, bf16[8,60,512]{2,1,0:T(8,128)(2,1)S(1)}, f32[8,60,512]{2,1,0:T(8,128)S(1)}, f32[8,60,512]{2,1,0:T(8,128)}, /*index=5*/s32[]{:T(128)}) while((s32[]{:T(128)}, f32[60,512]{1,0:T(8,128)S(1)}, bf16[8,60,512]{2,1,0:T(8,128)(2,1)S(1)}, f32[8,60,512]{2,1,0:T(8,128)S(1)}, ...), condition=%wide.region_19.21_spmd, body=%wide.region_18.20_spmd.sunk | while | flops 61442 | bytes 647241 | solution.py:109
  (330 shorter events, 191.9 us)
Async XLA Ops:
  7.2 89.4 %copy-start = (f32[60,60]{1,0:T(8,128)S(1)}, f32[60,60]{1,0:T(8,128)}, u32[]{:S(2)}) copy-start(f32[60,60]{1,0:T(8,128)} %param.40) | copy-start | bytes 43204
  9.6 23.1 %collective-permute-start = (f32[8,60,192]{2,0,1:T(8,128)}, f32[8,60,192]{2,0,1:T(8,128)S(1)}, u32[]{:S(2)}, u32[]{:S(2)}) collective-permute-start(f32[8,60,192]{2,0,1:T(8,128)} %get-tuple-element.526), channel_id=1, source_target_pairs={{0,4},{4,8},{8,12},{12,16},{16,20},{20,24},{24,28},{28,0},{1,5},{5... | collective-permute-start | bytes 1105928 | tf_op jit(solution)/shard_map/ppermute | solution.py:26
  10.0 22.6 %collective-permute-start.1 = (f32[8,60,192]{2,0,1:T(8,128)}, f32[8,60,192]{2,0,1:T(8,128)S(1)}, u32[]{:S(2)}, u32[]{:S(2)}) collective-permute-start(f32[8,60,192]{2,0,1:T(8,128)} %get-tuple-element.527), channel_id=1, source_target_pairs={{4,0},{8,4},{12,8},{16,12},{20,16},{24,20},{28,24},{0,28},{5,1},{9... | collective-permute-start | bytes 1105928 | tf_op jit(solution)/shard_map/ppermute | solution.py:28
  15.4 81.2 %collective-permute-start.2 = (f32[60,512]{1,0:T(8,128)}, f32[60,512]{1,0:T(8,128)}, u32[]{:S(2)}, u32[]{:S(2)}) collective-permute-start(f32[60,512]{1,0:T(8,128)} %slice_bitcast_fusion.3), channel_id=1, source_target_pairs={{3,0},{0,1},{1,2},{2,3},{7,4},{4,5},{5,6},{6,7},{11,8},{8,9},{9,10... | collective-permute-start | bytes 368648 | tf_op jit(solution)/shard_map/ppermute | solution.py:16
  21.2 53.3 %copy-start.61 = (f32[1,512]{1,0:T(1,128)}, f32[1,512]{1,0:T(1,128)S(1)}, u32[]{:S(2)}) copy-start(f32[1,512]{1,0:T(1,128)S(1)} %get-tuple-element.545) | copy-start | bytes 6148
  21.2 59.8 %copy-start.55 = (f32[1,512]{1,0:T(1,128)}, f32[1,512]{1,0:T(1,128)S(1)}, u32[]{:S(2)}) copy-start(f32[1,512]{1,0:T(1,128)S(1)} %get-tuple-element.544) | copy-start | bytes 6148
  21.2 63.6 %copy-start.49 = (f32[1,512]{1,0:T(1,128)}, f32[1,512]{1,0:T(1,128)S(1)}, u32[]{:S(2)}) copy-start(f32[1,512]{1,0:T(1,128)S(1)} %get-tuple-element.543) | copy-start | bytes 6148
  21.2 67.8 %copy-start.43 = (f32[1,512]{1,0:T(1,128)}, f32[1,512]{1,0:T(1,128)S(1)}, u32[]{:S(2)}) copy-start(f32[1,512]{1,0:T(1,128)S(1)} %get-tuple-element.542) | copy-start | bytes 6148
  21.2 71.5 %copy-start.41 = (f32[1,512]{1,0:T(1,128)}, f32[1,512]{1,0:T(1,128)S(1)}, u32[]{:S(2)}) copy-start(f32[1,512]{1,0:T(1,128)S(1)} %get-tuple-element.541) | copy-start | bytes 6148
  21.3 40.1 %copy-start.75 = (s32[1024]{0:T(1024)}, s32[1024]{0:T(1024)S(1)}, u32[]{:S(2)}) copy-start(s32[1024]{0:T(1024)S(1)} %pad_clamp_fusion.1) | copy-start | bytes 12292
  22.6 58.4 %copy-start.63 = (f32[1,512]{1,0:T(1,128)}, f32[1,512]{1,0:T(1,128)S(1)}, u32[]{:S(2)}) copy-start(f32[1,512]{1,0:T(1,128)S(1)} %get-tuple-element.534) | copy-start | bytes 6148
  22.6 62.2 %copy-start.57 = (f32[1,512]{1,0:T(1,128)}, f32[1,512]{1,0:T(1,128)S(1)}, u32[]{:S(2)}) copy-start(f32[1,512]{1,0:T(1,128)S(1)} %get-tuple-element.533) | copy-start | bytes 6148
  22.6 62.2 %copy-start.59 = (f32[1,512]{1,0:T(1,128)}, f32[1,512]{1,0:T(1,128)S(1)}, u32[]{:S(2)}) copy-start(f32[1,512]{1,0:T(1,128)S(1)} %get-tuple-element.556) | copy-start | bytes 6148
  22.6 66.4 %copy-start.51 = (f32[1,512]{1,0:T(1,128)}, f32[1,512]{1,0:T(1,128)S(1)}, u32[]{:S(2)}) copy-start(f32[1,512]{1,0:T(1,128)S(1)} %get-tuple-element.532) | copy-start | bytes 6148
  22.6 66.4 %copy-start.53 = (f32[1,512]{1,0:T(1,128)}, f32[1,512]{1,0:T(1,128)S(1)}, u32[]{:S(2)}) copy-start(f32[1,512]{1,0:T(1,128)S(1)} %get-tuple-element.557) | copy-start | bytes 6148
  22.6 70.2 %copy-start.45 = (f32[1,512]{1,0:T(1,128)}, f32[1,512]{1,0:T(1,128)S(1)}, u32[]{:S(2)}) copy-start(f32[1,512]{1,0:T(1,128)S(1)} %get-tuple-element.531) | copy-start | bytes 6148
  22.6 70.2 %copy-start.47 = (f32[1,512]{1,0:T(1,128)}, f32[1,512]{1,0:T(1,128)S(1)}, u32[]{:S(2)}) copy-start(f32[1,512]{1,0:T(1,128)S(1)} %get-tuple-element.558) | copy-start | bytes 6148
  29.2 38.8 %copy-start.77 = (s32[1024]{0:T(1024)}, s32[1024]{0:T(1024)S(1)}, u32[]{:S(2)}) copy-start(s32[1024]{0:T(1024)S(1)} %pad_clamp_fusion) | copy-start | bytes 12292
  152.4 38.7 %all-reduce.6.cloned.1.call-start = ((), (), s32[]{:S(2)}) async-start(), calls=%async_computation.1 | async-start | bytes 524288 | tf_op jit(solution)/shard_map/psum | solution.py:49
  212.6 13.3 %collective-permute-start.3 = (f32[8,60,192]{2,1,0:T(8,128)S(1)}, f32[8,60,192]{2,1,0:T(8,128)S(1)}, u32[]{:S(2)}, u32[]{:S(2)}) collective-permute-start(f32[8,60,192]{2,1,0:T(8,128)S(1)} %get-tuple-element.524), channel_id=1, source_target_pairs={{0,4},{4,8},{8,12},{12,16},{16,20},{20,24},{24,28},{28,0},{1,5},{5... | collective-permute-start | bytes 1105928 | tf_op jit(solution)/shard_map/ppermute | solution.py:26
  212.7 13.3 %collective-permute-start.4 = (f32[8,60,192]{2,1,0:T(8,128)S(1)}, f32[8,60,192]{2,1,0:T(8,128)S(1)}, u32[]{:S(2)}, u32[]{:S(2)}) collective-permute-start(f32[8,60,192]{2,1,0:T(8,128)S(1)} %get-tuple-element.525), channel_id=1, source_target_pairs={{4,0},{8,4},{12,8},{16,12},{20,16},{24,20},{28,24},{0,28},{5,1},{9... | collective-permute-start | bytes 1105928 | tf_op jit(solution)/shard_map/ppermute | solution.py:28
  215.3 89.5 %collective-permute-start.5 = (f32[60,512]{1,0:T(8,128)S(1)}, f32[60,512]{1,0:T(8,128)}, u32[]{:S(2)}, u32[]{:S(2)}) collective-permute-start(f32[60,512]{1,0:T(8,128)S(1)} %slice_bitcast_fusion.2), channel_id=1, source_target_pairs={{3,0},{0,1},{1,2},{2,3},{7,4},{4,5},{5,6},{6,7},{11,8},{8,9},{9,10... | collective-permute-start | bytes 368648 | tf_op jit(solution)/shard_map/ppermute | solution.py:16
  334.4 38.0 %all-reduce.4.cloned.1.call-start = ((), (), s32[]{:S(2)}) async-start(), calls=%async_computation | async-start | bytes 262144 | tf_op jit(solution)/shard_map/psum | solution.py:98
  335.3 46.3 %copy-start.2 = (f32[8,60,512]{2,1,0:T(8,128)S(1)}, f32[8,60,512]{2,1,0:T(8,128)}, u32[]{:S(2)}) copy-start(f32[8,60,512]{2,1,0:T(8,128)} %copy-done.1) | copy-start | bytes 2949124
  (78 other events, 536.0 us)
Sparse Core Ops, SparseCore 0:
  156.2 34.8 all-reduce.5
  338.2 34.1 all-reduce.3
where the time goes:
time: 397 us; the launch traced here: 391 us
  local copies, waits for them, and re-layouts  95.8 us (24%)
  other arithmetic  85.6 us (22%)
  waiting for transfers between devices  78.5 us (20%)
  matrix products  55.7 us (14%)
  blocking collectives  48.4 us (12%)
  between operations  16.7 us (4%)
  starting transfers between devices  9.72 us (2%)
    gather x20, local copies, waits for them, and re-layouts, operate(): picked = jnp.take(extended, place[face_id], axis=2)  73.6 us
    all_gather x3, blocking collectives, entering_2(): pieces = lax.all_gather(value, axis)  48.4 us
    dot_general x10, matrix products, operate(): jnp.einsum('ij,sje->sie', face_ops[face_id], stacked, precision=HIGH)  38.2 us
    psum x1, waiting for transfers between devices, broadcast(): return lax.psum(kept, axis)  35 us
    psum x1, waiting for transfers between devices, periodic_scan(): everything = lax.psum(scaled, 'slab')  34.2 us
    dynamic_update_slice x16, other arithmetic, periodic_scan(): _, solved = lax.scan(advance, entering, (factor, offset))  20.9 us
    add x16, other arithmetic, compose(): return (step_gain * state + step_offset, None)  19.8 us
    mul x10, other arithmetic, operate(): picked * masks[face_id, rotation][None, None, :]  17.5 us
  transfers between devices with their start and end apart: 8, of which 3 were waited for; matrix products, arithmetic and copies ran while one was open for 42% of the time, Pallas kernels for 0%

commit v1 on v0

v1 whole, which is shorter than its diff:
```python
import functools

import jax
import jax.numpy as jnp
from jax import lax
from jax.experimental import pallas as pl
from jax.experimental.pallas import tpu as pltpu
from jax.sharding import PartitionSpec as P

SECTIONS = 2
RELAX = 0.8
F32 = jnp.float32
BF16 = jnp.bfloat16
MESH = pl.DeviceIdType.MESH


def dot(left, right):
    return jnp.dot(left, right, preferred_element_type=F32)


def split(value):
    high = value.astype(BF16)
    return high, (value - high.astype(F32)).astype(BF16)


def smoother(
    n_sector, n_slab, dof, row,
    iterate, right_side, geometry, scale, rates, index, side, orientation, counts,
    volume_ops, face_ops, time_coupling, precondition,
    smoothed, final_residual,
    cells, onehot, edge_onehot, picked, masks, face_f32, face_w, volume_f32, volume_w, pre_f32, pre_w,
    residual_parts, source, inverse, rate_rows, closing, state,
    before, after, previous, gain_out, gain_in, offset_out, offset_in,
    send_sems, recv_sems,
):
    slabs, _, count = iterate.shape
    faces = index.shape[0]
    half = count // 2
    width = 3 * count // 8
    my_sector, my_slab = lax.axis_index("sector"), lax.axis_index("slab")
    next_sector = lax.rem(my_sector + 1, n_sector)
    prev_sector = lax.rem(my_sector + n_sector - 1, n_sector)
    ahead = [None] + [lax.rem(my_slab + m, n_slab) for m in range(1, n_slab)]

    barrier = pltpu.get_barrier_semaphore()
    for target in (next_sector, prev_sector):
        pl.semaphore_signal(barrier, inc=1, device_id={"sector": target}, device_id_type=MESH)
    for m in range(1, n_slab):
        pl.semaphore_signal(barrier, inc=1, device_id={"slab": ahead[m]}, device_id_type=MESH)

    def remote(src, dst, slot, target):
        return pltpu.make_async_remote_copy(
            src_ref=src, dst_ref=dst, send_sem=send_sems.at[slot], recv_sem=recv_sems.at[slot],
            device_id=target, device_id_type=MESH,
        )

    per_section = 3 + n_slab - 1
    gain_base = SECTIONS * per_section

    cells[...] = jnp.zeros_like(cells)

    def to_cells(s, carry):
        cells[s + 1, 0:dof, :] = iterate[s].astype(BF16)
        return carry

    lax.fori_loop(0, slabs, to_cells, 0)
    total = 1.0 / scale[0:1, :]
    inverse[0:1, :] = total
    for s in range(1, slabs):
        one = 1.0 / scale[s : s + 1, :]
        inverse[s : s + 1, :] = one
        total = total * one
    gain_out[...] = jnp.broadcast_to(total, gain_out.shape)

    pl.semaphore_wait(barrier, 2 + n_slab - 1)

    def field_copies(section):
        base = section * per_section
        inner = cells.at[pl.ds(1, slabs)]
        return [
            remote(inner.at[:, :, pl.ds(half, half)], before.at[section], base, {"sector": next_sector}),
            remote(inner.at[:, :, pl.ds(0, half)], after.at[section], base + 1, {"sector": prev_sector}),
            remote(cells.at[slabs], previous.at[section], base + 2, {"slab": ahead[1]}),
        ]

    def offset_copies(section):
        base = section * per_section + 2
        return [
            remote(offset_out.at[section], offset_in.at[section, m], base + m, {"slab": ahead[m]})
            for m in range(1, n_slab)
        ]

    gain_copies = [
        remote(gain_out, gain_in.at[m], gain_base + m - 1, {"slab": ahead[m]}) for m in range(1, n_slab)
    ]

    field_now = field_copies(0)
    for copy in field_now:
        copy.start()
    for copy in gain_copies:
        copy.start()

    rows = lax.broadcasted_iota(jnp.int32, (count, count), 0)
    side_first = side[0:1, :]
    index_first = index[0:1, :]
    own_first = jnp.where(side_first == 0, index_first, -1)
    onehot[0] = jnp.where(rows == own_first, 1.0, 0.0).astype(BF16)

    def build(f, carry):
        onehot[f] = jnp.where(rows == index[pl.ds(f, 1), :], 1.0, 0.0).astype(BF16)
        return carry

    lax.fori_loop(1, faces, build, 0)
    edge_rows = lax.broadcasted_iota(jnp.int32, (half, half), 0)
    from_before = jnp.where(side_first < 0, index_first - half, -1)[:, 0:half]
    from_after = jnp.where(side_first > 0, index_first, -1)[:, half:count]
    edge_onehot[0] = jnp.where(edge_rows == from_before, 1.0, 0.0).astype(BF16)
    edge_onehot[1] = jnp.where(edge_rows == from_after, 1.0, 0.0).astype(BF16)
    for f in range(faces):
        turned = orientation[f : f + 1, :]
        for o in range(3):
            mask = jnp.where(turned == o, 1.0, 0.0)
            masks[3 * f + o] = jnp.broadcast_to(mask, (row, count)).astype(BF16)

    face_f32[...] = jnp.zeros_like(face_f32)
    for f in range(faces):
        for o in range(3):
            at = (3 * f + o) * row
            face_f32[0:dof, at : at + dof] = face_ops[f, :, o * dof : (o + 1) * dof]
    high, low = split(face_f32[...])
    face_w[0:row, :] = high
    face_w[row : 2 * row, :] = low
    volume_f32[...] = jnp.zeros_like(volume_f32)
    volume_f32[0:dof, 0:dof] = -time_coupling[...]
    for d in range(4):
        volume_f32[d * row : d * row + dof, row : row + dof] = volume_ops[d]
    high, low = split(volume_f32[...])
    volume_w[:, 0 : 2 * row] = high
    volume_w[:, 2 * row : 4 * row] = low
    pre_f32[...] = jnp.zeros_like(pre_f32)
    for part in range(3):
        pre_f32[0:dof, part * row : part * row + dof] = precondition[...]
    high, low = split(pre_f32[...])
    part_of = lax.broadcasted_iota(jnp.int32, pre_f32.shape, 1) // row
    pre_w[...] = jnp.where(part_of == 1, low.astype(F32), high.astype(F32)).astype(BF16)
    residual_parts[...] = jnp.zeros_like(residual_parts)

    diagonal = lax.broadcasted_iota(jnp.int32, (dof, dof), 0) == lax.broadcasted_iota(jnp.int32, (dof, dof), 1)
    column = jnp.sum(jnp.where(diagonal, jnp.broadcast_to(rates[...], (dof, dof)), 0.0), axis=1, keepdims=True)
    rate_rows[...] = jnp.broadcast_to(column, (dof, count))
    power = column
    for _ in range(slabs - 1):
        power = power * column

    slots = lax.broadcasted_iota(jnp.int32, (1, count), 1)
    live = jnp.where((slots < counts[0] - width) | (slots >= count - width), 1.0, 0.0)
    offset_out[...] = jnp.zeros_like(offset_out)

    for section in range(SECTIONS):
        last = section == SECTIONS - 1
        flat = slabs * row

        def gather(f, carry):
            values = cells[pl.ds(1, slabs)].reshape(flat, count)
            picked[f] = dot(values, onehot[f]).astype(BF16).reshape(slabs, row, count)
            return carry

        lax.fori_loop(0, faces, gather, 0)
        for copy in field_now:
            copy.wait()
        cells[0] = previous[section]
        left = dot(before[section].reshape(flat, half), edge_onehot[0]).astype(BF16)
        picked[0, :, :, 0:half] = picked[0, :, :, 0:half] + left.reshape(slabs, row, half)
        right = dot(after[section].reshape(flat, half), edge_onehot[1]).astype(BF16)
        picked[0, :, :, half:count] = picked[0, :, :, half:count] + right.reshape(slabs, row, half)

        state[...] = jnp.zeros_like(state)

        def apply(s, carry):
            pair = cells[pl.ds(s, 2)].reshape(2 * row, count)
            terms = dot(volume_w[...], jnp.concatenate([pair, pair], axis=0))
            applied = terms[0:row]
            for d in range(3):
                applied = applied + geometry[s, d : d + 1, :] * terms[(d + 1) * row : (d + 2) * row]
            blocks = []
            for f in range(faces):
                block = picked[f, s]
                for o in range(3):
                    blocks.append(block * masks[3 * f + o])
            flux = dot(face_w[...], jnp.concatenate(blocks, axis=0))
            applied = applied + flux[0:row] + flux[row : 2 * row]
            residual = live * (right_side[s] - applied[0:dof])
            if last:
                final_residual[s] = residual
            high, low = split(residual)
            residual_parts[0:dof, :] = high
            residual_parts[row : row + dof, :] = high
            residual_parts[2 * row : 2 * row + dof, :] = low
            rounded = dot(pre_w[...], residual_parts[...])[0:dof].astype(BF16)
            source[s, 0:dof, :] = rounded
            state[...] = inverse[pl.ds(s, 1), :] * (rate_rows[...] * state[...] + rounded.astype(F32))
            return carry

        lax.fori_loop(0, slabs, apply, 0)
        offset_out[section, 0:dof, :] = state[...]
        offsets = offset_copies(section)
        for copy in offsets:
            copy.start()
        if section == 0:
            for copy in gain_copies:
                copy.wait()
            whole = power * gain_out[0:1, :]
            for m in range(1, n_slab):
                whole = whole * (power * gain_in[m, 0:1, :])
            closing[...] = 1.0 / (1.0 - whole)
        for copy in offsets:
            copy.wait()
        entering = state[...]
        for m in range(n_slab - 1, 0, -1):
            entering = offset_in[section, m, 0:dof, :] + (power * gain_in[m, 0:1, :]) * entering
        state[...] = entering * closing[...]
        field = iterate if section == 0 else smoothed

        def advance(s, carry):
            value = inverse[pl.ds(s, 1), :] * (rate_rows[...] * state[...] + source[s, 0:dof, :].astype(F32))
            state[...] = value
            updated = field[s] + RELAX * value.astype(BF16).astype(F32)
            smoothed[s] = updated
            if not last:
                cells[s + 1, 0:dof, :] = updated.astype(BF16)
            return carry

        lax.fori_loop(0, slabs, advance, 0)
        if not last:
            field_now = field_copies(section + 1)
            for copy in field_now:
                copy.start()


def on_device(
    n_sector, n_slab,
    iterate, right_side, geometry, temporal_block_scale, decay_rates, neighbour_index,
    neighbour_side, orientation, sector_counts, volume_ops, face_ops, time_coupling, precondition,
):
    slabs, dof, count = iterate.shape
    faces = neighbour_index.shape[0]
    row = -(-dof // 16) * 16
    half = count // 2
    vmem = pl.BlockSpec(memory_space=pltpu.VMEM)
    smem = pl.BlockSpec(memory_space=pltpu.SMEM)
    copies = SECTIONS * (3 + n_slab - 1) + n_slab - 1
    out = jax.ShapeDtypeStruct(iterate.shape, F32)
    return pl.pallas_call(
        functools.partial(smoother, n_sector, n_slab, dof, row),
        out_shape=(out, out),
        in_specs=[vmem] * 8 + [smem] + [vmem] * 4,
        out_specs=(vmem, vmem),
        scratch_shapes=[
            pltpu.VMEM((slabs + 1, row, count), BF16),
            pltpu.VMEM((faces, count, count), BF16),
            pltpu.VMEM((2, half, half), BF16),
            pltpu.VMEM((faces, slabs, row, count), BF16),
            pltpu.VMEM((3 * faces, row, count), BF16),
            pltpu.VMEM((row, 3 * faces * row), F32),
            pltpu.VMEM((2 * row, 3 * faces * row), BF16),
            pltpu.VMEM((4 * row, 2 * row), F32),
            pltpu.VMEM((4 * row, 4 * row), BF16),
            pltpu.VMEM((row, 3 * row), F32),
            pltpu.VMEM((row, 3 * row), BF16),
            pltpu.VMEM((3 * row, count), BF16),
            pltpu.VMEM((slabs, row, count), BF16),
            pltpu.VMEM((slabs, count), F32),
            pltpu.VMEM((dof, count), F32),
            pltpu.VMEM((dof, count), F32),
            pltpu.VMEM((dof, count), F32),
            pltpu.VMEM((SECTIONS, slabs, row, half), BF16),
            pltpu.VMEM((SECTIONS, slabs, row, half), BF16),
            pltpu.VMEM((SECTIONS, row, count), BF16),
            pltpu.VMEM((8, count), F32),
            pltpu.VMEM((n_slab, 8, count), F32),
            pltpu.VMEM((SECTIONS, row, count), F32),
            pltpu.VMEM((SECTIONS, n_slab, row, count), F32),
            pltpu.SemaphoreType.DMA((copies,)),
            pltpu.SemaphoreType.DMA((copies,)),
        ],
        compiler_params=pltpu.CompilerParams(
            collective_id=0, has_side_effects=True, vmem_limit_bytes=56 << 20
        ),
    )(
        iterate, right_side, geometry, temporal_block_scale, decay_rates[None, :], neighbour_index,
        neighbour_side, orientation, sector_counts, volume_ops, face_ops, time_coupling, precondition,
    )


def solution(mesh):
    in_specs = (
        P("slab", None, "sector"),
        P("slab", None, "sector"),
        P("slab", None, "sector"),
        P("slab", "sector"),
        P(),
        P(None, "sector"),
        P(None, "sector"),
        P(None, "sector"),
        P("sector"),
        P(),
        P(),
        P(),
        P(),
    )
    out_specs = (P("slab", None, "sector"), P("slab", None, "sector"))
    body = functools.partial(on_device, mesh.shape["sector"], mesh.shape["slab"])
    return jax.shard_map(body, mesh=mesh, in_specs=in_specs, out_specs=out_specs, check_vma=False)
```

time: 397 us -> 69.4 us (0.17); the launches traced: 391 us -> 68.5 us
  other arithmetic: 85.6 us -> 0 us
  local copies, waits for them, and re-layouts: 95.8 us -> 11.8 us
  waiting for transfers between devices: 78.5 us -> 0 us
  matrix products: 55.7 us -> 0 us
  Pallas kernels: 0 us -> 55.4 us
  blocking collectives: 48.4 us -> 0 us
  between operations: 16.7 us -> 1.3 us
  starting transfers between devices: 9.72 us -> 0 us
    gather x20 -> x0, local copies, waits for them, and re-layouts: 73.6 us -> none  [operate(): picked = jnp.take(extended, place[face_id], axis=2)]
    psum x2 -> x0, waiting for transfers between devices: 69.2 us -> none  [the longest x1 35 us: broadcast(): return lax.psum(kept, axis)]
    dot_general x16 -> x0, matrix products: 55.7 us -> none  [the longest x10 38.2 us: operate(): jnp.einsum('ij,sje->sie', face_ops[face_id], stacked, precision=HIGH)]
    pallas_call x0 -> x1, Pallas kernels: none -> 55.4 us  [on_device(): pl.pallas_call(functools.partial(smoother, n_sector, n_slab, dof, row), o...]
    all_gather x3 -> x0, blocking collectives: 48.4 us -> none  [entering_2(): pieces = lax.all_gather(value, axis)]
    add x20 -> x0, other arithmetic: 24.3 us -> none  [the longest x16 19.8 us: compose(): return (step_gain * state + step_offset, None)]
    dynamic_update_slice x16 -> x0, other arithmetic: 20.9 us -> none  [periodic_scan(): _, solved = lax.scan(advance, entering, (factor, offset))]
    mul x10 -> x0, other arithmetic: 17.5 us -> none  [operate(): picked * masks[face_id, rotation][None, None, :]]
  transfers between devices with their start and end apart: 8 -> 0, of which waited for: 3 -> 0; matrix products, arithmetic and copies ran while one was open for 42% -> 0% of each run, Pallas kernels for 0% -> 0%
where the time goes in v1:
time: 69.4 us; the launch traced here: 68.5 us
  Pallas kernels  55.4 us (80%)
  local copies, waits for them, and re-layouts  11.8 us (17%)
  between operations  1.3 us (2%)
    pallas_call x1, Pallas kernels, on_device(): pl.pallas_call(functools.partial(smoother, n_sector, n_slab, dof, row), o...  55.4 us
    unnamed x8, local copies, waits for them, and re-layouts  7.46 us
    pallas_call x2, local copies, waits for them, and re-layouts, on_device(): pl.pallas_call(functools.partial(smoother, n_sector, n_slab, dof, row), o...  4.35 us

profile of v1, /device:TPU:0, one launch (start us, length us, event | category | flops | bytes accessed | tf_op | source)
XLA Modules:
  0.0 68.5 jit_solution(1354130413152082016)
XLA Ops:
  1.3 1.5 %copy.17.geometry = f32[8,3,512]{2,1,0:T(4,128)} copy(f32[8,3,512]{2,0,1:T(8,128)} %param.15) | data formatting | bytes 98304 | tf_op args[2]
  2.7 1.6 %copy.18.volume_ops = f32[4,60,60]{2,1,0:T(8,128)} copy(f32[4,60,60]{2,0,1:T(4,128)} %param.22) | data formatting | bytes 115200 | tf_op args[9]
  4.3 0.0 copy-start.1
  4.3 2.8 %copy.15.iterate = f32[8,60,512]{2,1,0:T(8,128)} copy(f32[8,60,512]{2,0,1:T(8,128)} %param.13) | data formatting | bytes 1966080 | tf_op args[0]
  7.1 0.0 copy-done.1
  7.1 1.6 %copy.16.right_side = f32[8,60,512]{2,1,0:T(8,128)} copy(f32[8,60,512]{2,0,1:T(8,128)S(1)} %copy-done.1) | data formatting | bytes 1966080 | tf_op args[1]
  8.7 55.4 %shard_map.140 = (f32[8,60,512]{2,1,0:T(8,128)}, f32[8,60,512]{2,1,0:T(8,128)}) custom-call(f32[8,60,512]{2,1,0:T(8,128)} %copy.15.iterate, f32[8,60,512]{2,1,0:T(8,128)} %copy.16.right_side, f32[8,3,512]{2,1,0:T(4,128)} %copy.17.geometry, f32[8,512]{1,0:T(8,128)} %scale.1, f32[1,60]{1,0:T(1,128)} %bitcast.1, s32[5,512]{1,0:T(8,128)} %index.1, ...), custom_call_target="tpu_custom_call" | custom-call | tf_op jit(solution)/shard_map/pallas_call | solution.py:253
  64.1 0.0 copy-start
  64.2 2.8 %copy.19 = f32[8,60,512]{2,0,1:T(8,128)} copy(f32[8,60,512]{2,1,0:T(8,128)} %get-tuple-element.2) | data formatting | bytes 1966080 | tf_op jit(solution)/shard_map/pallas_call | solution.py:253
  67.0 0.0 copy-done
  67.0 1.5 %copy.20 = f32[8,60,512]{2,0,1:T(8,128)} copy(f32[8,60,512]{2,1,0:T(8,128)S(1)} %copy-done) | data formatting | bytes 1966080 | tf_op jit(solution)/shard_map/pallas_call | solution.py:253
Async XLA Ops:
  4.3 2.8 %copy-start.1 = (f32[8,60,512]{2,0,1:T(8,128)S(1)}, f32[8,60,512]{2,0,1:T(8,128)}, u32[]{:S(2)}) copy-start(f32[8,60,512]{2,0,1:T(8,128)} %param.14) | copy-start | bytes 2949124
  64.1 2.8 %copy-start = (f32[8,60,512]{2,1,0:T(8,128)S(1)}, f32[8,60,512]{2,1,0:T(8,128)}, u32[]{:S(2)}) copy-start(f32[8,60,512]{2,1,0:T(8,128)} %get-tuple-element.3) | copy-start | bytes 2949124

commit v2 on v1

--- a/solution.py
+++ b/solution.py
@@ -9,6 +9,7 @@
 
 SECTIONS = 2
 RELAX = 0.8
+LANES = 128
 F32 = jnp.float32
 BF16 = jnp.bfloat16
 MESH = pl.DeviceIdType.MESH
@@ -24,16 +25,17 @@
 
 
 def smoother(
-    n_sector, n_slab, dof, row,
+    n_sector, n_slab, slabs, dof, row,
     iterate, right_side, geometry, scale, rates, index, side, orientation, counts,
     volume_ops, face_ops, time_coupling, precondition,
     smoothed, final_residual,
-    cells, onehot, edge_onehot, picked, masks, face_f32, face_w, volume_f32, volume_w, pre_f32, pre_w,
+    cells, cells_low, onehot, edge_onehot, picked, picked_low, masks, face_f32, face_w, volume_f32, volume_w, pre_f32, pre_w,
     residual_parts, source, inverse, rate_rows, closing, state,
     before, after, previous, gain_out, gain_in, offset_out, offset_in,
     send_sems, recv_sems,
 ):
-    slabs, _, count = iterate.shape
+    count = index.shape[1]
+    tiles = count // LANES
     faces = index.shape[0]
     half = count // 2
     width = 3 * count // 8
@@ -58,9 +60,22 @@
     gain_base = SECTIONS * per_section
 
     cells[...] = jnp.zeros_like(cells)
+    cells_low[...] = jnp.zeros_like(cells_low)
+
+    def lines(s, tile):
+        return pl.ds(tile * slabs + s, dof, stride=tiles * slabs), slice(None)
+
+    def load_slab(ref, s):
+        return jnp.concatenate([ref[lines(s, tile)] for tile in range(tiles)], axis=1)
+
+    def store_slab(ref, s, value):
+        for tile in range(tiles):
+            ref[lines(s, tile)] = value[:, tile * LANES : (tile + 1) * LANES]
 
     def to_cells(s, carry):
-        cells[s + 1, 0:dof, :] = iterate[s].astype(BF16)
+        high, low = split(load_slab(iterate, s))
+        cells[s + 1, 0:dof, :] = high
+        cells_low[s + 1, 0:dof, :] = low
         return carry
 
     lax.fori_loop(0, slabs, to_cells, 0)
@@ -133,10 +148,11 @@
     volume_f32[...] = jnp.zeros_like(volume_f32)
     volume_f32[0:dof, 0:dof] = -time_coupling[...]
     for d in range(4):
-        volume_f32[d * row : d * row + dof, row : row + dof] = volume_ops[d]
+        volume_f32[d * row : d * row + dof, row : row + dof] = volume_ops[:, d, :]
     high, low = split(volume_f32[...])
     volume_w[:, 0 : 2 * row] = high
     volume_w[:, 2 * row : 4 * row] = low
+    volume_w[:, 4 * row : 6 * row] = high
     pre_f32[...] = jnp.zeros_like(pre_f32)
     for part in range(3):
         pre_f32[0:dof, part * row : part * row + dof] = precondition[...]
@@ -163,6 +179,8 @@
         def gather(f, carry):
             values = cells[pl.ds(1, slabs)].reshape(flat, count)
             picked[f] = dot(values, onehot[f]).astype(BF16).reshape(slabs, row, count)
+            values = cells_low[pl.ds(1, slabs)].reshape(flat, count)
+            picked_low[f] = dot(values, onehot[f]).astype(BF16).reshape(slabs, row, count)
             return carry
 
         lax.fori_loop(0, faces, gather, 0)
@@ -178,20 +196,23 @@
 
         def apply(s, carry):
             pair = cells[pl.ds(s, 2)].reshape(2 * row, count)
-            terms = dot(volume_w[...], jnp.concatenate([pair, pair], axis=0))
+            pair_low = cells_low[pl.ds(s, 2)].reshape(2 * row, count)
+            terms = dot(volume_w[...], jnp.concatenate([pair, pair, pair_low], axis=0))
             applied = terms[0:row]
             for d in range(3):
-                applied = applied + geometry[s, d : d + 1, :] * terms[(d + 1) * row : (d + 2) * row]
-            blocks = []
+                applied = applied + geometry[d, pl.ds(s, 1), :] * terms[(d + 1) * row : (d + 2) * row]
+            blocks, blocks_low = [], []
             for f in range(faces):
-                block = picked[f, s]
+                block, block_low = picked[f, s], picked_low[f, s]
                 for o in range(3):
                     blocks.append(block * masks[3 * f + o])
+                    blocks_low.append(block_low * masks[3 * f + o])
             flux = dot(face_w[...], jnp.concatenate(blocks, axis=0))
-            applied = applied + flux[0:row] + flux[row : 2 * row]
-            residual = live * (right_side[s] - applied[0:dof])
+            flux_low = dot(face_w[0:row, :], jnp.concatenate(blocks_low, axis=0))
+            applied = applied + flux[0:row] + flux[row : 2 * row] + flux_low
+            residual = live * (load_slab(right_side, s) - applied[0:dof])
             if last:
-                final_residual[s] = residual
+                store_slab(final_residual, s, residual)
             high, low = split(residual)
             residual_parts[0:dof, :] = high
             residual_parts[row : row + dof, :] = high
@@ -202,7 +223,7 @@
             return carry
 
         lax.fori_loop(0, slabs, apply, 0)
-        offset_out[section, 0:dof, :] = state[...]
+        offset_out[section, 0:dof, :] = state[...].astype(BF16)
         offsets = offset_copies(section)
         for copy in offsets:
             copy.start()
@@ -217,17 +238,19 @@
             copy.wait()
         entering = state[...]
         for m in range(n_slab - 1, 0, -1):
-            entering = offset_in[section, m, 0:dof, :] + (power * gain_in[m, 0:1, :]) * entering
+            entering = offset_in[section, m, 0:dof, :].astype(F32) + (power * gain_in[m, 0:1, :]) * entering
         state[...] = entering * closing[...]
         field = iterate if section == 0 else smoothed
 
         def advance(s, carry):
             value = inverse[pl.ds(s, 1), :] * (rate_rows[...] * state[...] + source[s, 0:dof, :].astype(F32))
             state[...] = value
-            updated = field[s] + RELAX * value.astype(BF16).astype(F32)
-            smoothed[s] = updated
+            updated = load_slab(field, s) + RELAX * value.astype(BF16).astype(F32)
+            store_slab(smoothed, s, updated)
             if not last:
-                cells[s + 1, 0:dof, :] = updated.astype(BF16)
+                high, low = split(updated)
+                cells[s + 1, 0:dof, :] = high
+                cells_low[s + 1, 0:dof, :] = low
             return carry
 
         lax.fori_loop(0, slabs, advance, 0)
@@ -246,25 +269,37 @@
     faces = neighbour_index.shape[0]
     row = -(-dof // 16) * 16
     half = count // 2
+    tiles = count // LANES
     vmem = pl.BlockSpec(memory_space=pltpu.VMEM)
     smem = pl.BlockSpec(memory_space=pltpu.SMEM)
     copies = SECTIONS * (3 + n_slab - 1) + n_slab - 1
-    out = jax.ShapeDtypeStruct(iterate.shape, F32)
-    return pl.pallas_call(
-        functools.partial(smoother, n_sector, n_slab, dof, row),
+
+    def by_dof(value):
+        lined = value.transpose(1, 0, 2).reshape(dof, slabs, tiles, LANES)
+        return lined.transpose(0, 2, 1, 3).reshape(dof * tiles * slabs, LANES)
+
+    def by_slab(value):
+        lined = value.reshape(dof, tiles, slabs, LANES).transpose(0, 2, 1, 3)
+        return lined.reshape(dof, slabs, count).transpose(1, 0, 2)
+
+    out = jax.ShapeDtypeStruct((dof * tiles * slabs, LANES), F32)
+    results = pl.pallas_call(
+        functools.partial(smoother, n_sector, n_slab, slabs, dof, row),
         out_shape=(out, out),
         in_specs=[vmem] * 8 + [smem] + [vmem] * 4,
         out_specs=(vmem, vmem),
         scratch_shapes=[
             pltpu.VMEM((slabs + 1, row, count), BF16),
+            pltpu.VMEM((slabs + 1, row, count), BF16),
             pltpu.VMEM((faces, count, count), BF16),
             pltpu.VMEM((2, half, half), BF16),
+            pltpu.VMEM((faces, slabs, row, count), BF16),
             pltpu.VMEM((faces, slabs, row, count), BF16),
             pltpu.VMEM((3 * faces, row, count), BF16),
             pltpu.VMEM((row, 3 * faces * row), F32),
             pltpu.VMEM((2 * row, 3 * faces * row), BF16),
             pltpu.VMEM((4 * row, 2 * row), F32),
-            pltpu.VMEM((4 * row, 4 * row), BF16),
+            pltpu.VMEM((4 * row, 6 * row), BF16),
             pltpu.VMEM((row, 3 * row), F32),
             pltpu.VMEM((row, 3 * row), BF16),
             pltpu.VMEM((3 * row, count), BF16),
@@ -278,8 +313,8 @@
             pltpu.VMEM((SECTIONS, row, count), BF16),
             pltpu.VMEM((8, count), F32),
             pltpu.VMEM((n_slab, 8, count), F32),
-            pltpu.VMEM((SECTIONS, row, count), F32),
-            pltpu.VMEM((SECTIONS, n_slab, row, count), F32),
+            pltpu.VMEM((SECTIONS, row, count), BF16),
+            pltpu.VMEM((SECTIONS, n_slab, row, count), BF16),
             pltpu.SemaphoreType.DMA((copies,)),
             pltpu.SemaphoreType.DMA((copies,)),
         ],
@@ -287,9 +322,11 @@
             collective_id=0, has_side_effects=True, vmem_limit_bytes=56 << 20
         ),
     )(
-        iterate, right_side, geometry, temporal_block_scale, decay_rates[None, :], neighbour_index,
-        neighbour_side, orientation, sector_counts, volume_ops, face_ops, time_coupling, precondition,
+        by_dof(iterate), by_dof(right_side), geometry.transpose(1, 0, 2), temporal_block_scale,
+        decay_rates[None, :], neighbour_index, neighbour_side, orientation, sector_counts,
+        volume_ops.transpose(1, 0, 2), face_ops, time_coupling, precondition,
     )
+    return tuple(by_slab(value) for value in results)
 
 
 def solution(mesh):

time: 69.4 us -> 55.6 us (0.80); the launches traced: 68.5 us -> 55.4 us
  local copies, waits for them, and re-layouts: 11.8 us -> 3.24 us
  Pallas kernels: 55.4 us -> 50.9 us
    pallas_call x1, Pallas kernels: 55.4 us -> 50.9 us  [on_device(): pl.pallas_call(functools.partial(smoother, n_sector, n_slab, slabs, dof,...]
    pallas_call x2 -> x0, local copies, waits for them, and re-layouts: 4.35 us -> none  [on_device(): pl.pallas_call(functools.partial(smoother, n_sector, n_slab, dof, row), o...]
    unnamed x8 -> x4, local copies, waits for them, and re-layouts: 7.46 us -> 3.24 us
where the time goes in v2:
time: 55.6 us; the launch traced here: 55.4 us
  Pallas kernels  50.9 us (92%)
  local copies, waits for them, and re-layouts  3.24 us (6%)
  between operations  1.3 us (2%)
    pallas_call x1, Pallas kernels, on_device(): pl.pallas_call(functools.partial(smoother, n_sector, n_slab, slabs, dof,...  50.9 us
    unnamed x4, local copies, waits for them, and re-layouts  3.24 us

profile of v2, /device:TPU:0, one launch (start us, length us, event | category | flops | bytes accessed | tf_op | source)
XLA Modules:
  0.0 55.4 jit_solution(5733960425647781983)
XLA Ops:
  1.3 50.9 %shard_map.140 = (f32[1920,128]{1,0:T(8,128)}, f32[1920,128]{1,0:T(8,128)}) custom-call(f32[1920,128]{1,0:T(8,128)} %bitcast.31, f32[1920,128]{1,0:T(8,128)} %bitcast.32, f32[3,8,512]{2,1,0:T(8,128)} %bitcast.36, f32[8,512]{1,0:T(8,128)} %scale.1, f32[1,60]{1,0:T(1,128)} %bitcast.37, s32[5,512]{1,0:T(8,128)} %index.1, s32[5,512]{1,0:T(8,128)} %side.1, ...), custom_call_target="tpu_custom_call" | custom-call | tf_op jit(solution)/shard_map/pallas_call | solution.py:286
  52.2 0.0 copy-start
  52.2 2.3 %copy.18 = f32[8,60,512]{2,0,1:T(8,128)} copy(f32[8,60,512]{2,0,1:T(8,128)} %bitcast.34) | data formatting | bytes 1966080
  54.5 0.0 copy-done
  54.5 0.9 %copy.19 = f32[8,60,512]{2,0,1:T(8,128)} copy(f32[8,60,512]{2,0,1:T(8,128)S(1)} %bitcast.33) | data formatting | bytes 1966080
Async XLA Ops:
  52.2 2.3 %copy-start = (f32[1920,128]{1,0:T(8,128)S(1)}, f32[1920,128]{1,0:T(8,128)}, u32[]{:S(2)}) copy-start(f32[1920,128]{1,0:T(8,128)} %get-tuple-element.5) | copy-start | bytes 2949124

commit v3 on v2

--- a/solution.py
+++ b/solution.py
@@ -29,7 +29,7 @@
     iterate, right_side, geometry, scale, rates, index, side, orientation, counts,
     volume_ops, face_ops, time_coupling, precondition,
     smoothed, final_residual,
-    cells, cells_low, onehot, edge_onehot, picked, picked_low, masks, face_f32, face_w, volume_f32, volume_w, pre_f32, pre_w,
+    cells, cells_low, onehot, edge_onehot, picked, picked_low, partial, edge, masks, face_f32, face_w, volume_f32, volume_w, pre_f32, pre_w,
     residual_parts, source, inverse, rate_rows, closing, state,
     before, after, previous, gain_out, gain_in, offset_out, offset_in,
     send_sems, recv_sems,
@@ -56,7 +56,7 @@
             device_id=target, device_id_type=MESH,
         )
 
-    per_section = 3 + n_slab - 1
+    per_section = 3 + 2 * (n_slab - 1)
     gain_base = SECTIONS * per_section
 
     cells[...] = jnp.zeros_like(cells)
@@ -65,15 +65,15 @@
     def lines(s, tile):
         return pl.ds(tile * slabs + s, dof, stride=tiles * slabs), slice(None)
 
-    def load_slab(ref, s):
-        return jnp.concatenate([ref[lines(s, tile)] for tile in range(tiles)], axis=1)
-
-    def store_slab(ref, s, value):
-        for tile in range(tiles):
-            ref[lines(s, tile)] = value[:, tile * LANES : (tile + 1) * LANES]
+    def load_slab(ref, s, first, stop):
+        return jnp.concatenate([ref[lines(s, tile)] for tile in range(first, stop)], axis=1)
+
+    def store_slab(ref, s, value, first):
+        for tile in range(value.shape[1] // LANES):
+            ref[lines(s, first + tile)] = value[:, tile * LANES : (tile + 1) * LANES]
 
     def to_cells(s, carry):
-        high, low = split(load_slab(iterate, s))
+        high, low = split(load_slab(iterate, s, 0, tiles))
         cells[s + 1, 0:dof, :] = high
         cells_low[s + 1, 0:dof, :] = low
         return carry
@@ -98,10 +98,10 @@
             remote(cells.at[slabs], previous.at[section], base + 2, {"slab": ahead[1]}),
         ]
 
-    def offset_copies(section):
-        base = section * per_section + 2
+    def offset_copies(section, part):
+        base = section * per_section + 2 + part * (n_slab - 1)
         return [
-            remote(offset_out.at[section], offset_in.at[section, m], base + m, {"slab": ahead[m]})
+            remote(offset_out.at[section, part], offset_in.at[section, part, m], base + m, {"slab": ahead[m]})
             for m in range(1, n_slab)
         ]
 
@@ -184,15 +184,7 @@
             return carry
 
         lax.fori_loop(0, faces, gather, 0)
-        for copy in field_now:
-            copy.wait()
-        cells[0] = previous[section]
-        left = dot(before[section].reshape(flat, half), edge_onehot[0]).astype(BF16)
-        picked[0, :, :, 0:half] = picked[0, :, :, 0:half] + left.reshape(slabs, row, half)
-        right = dot(after[section].reshape(flat, half), edge_onehot[1]).astype(BF16)
-        picked[0, :, :, half:count] = picked[0, :, :, half:count] + right.reshape(slabs, row, half)
-
-        state[...] = jnp.zeros_like(state)
+        cells[0] = jnp.zeros_like(cells[0])
 
         def apply(s, carry):
             pair = cells[pl.ds(s, 2)].reshape(2 * row, count)
@@ -209,24 +201,50 @@
                     blocks_low.append(block_low * masks[3 * f + o])
             flux = dot(face_w[...], jnp.concatenate(blocks, axis=0))
             flux_low = dot(face_w[0:row, :], jnp.concatenate(blocks_low, axis=0))
-            applied = applied + flux[0:row] + flux[row : 2 * row] + flux_low
-            residual = live * (load_slab(right_side, s) - applied[0:dof])
-            if last:
-                store_slab(final_residual, s, residual)
-            high, low = split(residual)
-            residual_parts[0:dof, :] = high
-            residual_parts[row : row + dof, :] = high
-            residual_parts[2 * row : 2 * row + dof, :] = low
-            rounded = dot(pre_w[...], residual_parts[...])[0:dof].astype(BF16)
-            source[s, 0:dof, :] = rounded
-            state[...] = inverse[pl.ds(s, 1), :] * (rate_rows[...] * state[...] + rounded.astype(F32))
+            partial[s] = applied + flux[0:row] + flux[row : 2 * row] + flux_low
             return carry
 
         lax.fori_loop(0, slabs, apply, 0)
-        offset_out[section, 0:dof, :] = state[...].astype(BF16)
-        offsets = offset_copies(section)
-        for copy in offsets:
-            copy.start()
+        for copy in field_now:
+            copy.wait()
+        slab_before = previous[section]
+        weights = jnp.concatenate([volume_w[0:row, 0:row], volume_w[0:row, 2 * row : 3 * row]], axis=1)
+        partial[0] = partial[0] + dot(weights, jnp.concatenate([slab_before, slab_before], axis=0))
+        left = dot(before[section].reshape(flat, half), edge_onehot[0]).astype(BF16)
+        edge[:, :, 0:half] = left.reshape(slabs, row, half)
+        right = dot(after[section].reshape(flat, half), edge_onehot[1]).astype(BF16)
+        edge[:, :, half:count] = right.reshape(slabs, row, half)
+        state[...] = jnp.zeros_like(state)
+
+        offsets = []
+        for part in range(2):
+            lanes = slice(part * half, (part + 1) * half)
+            first, stop = part * tiles // 2, (part + 1) * tiles // 2
+
+            def finish(s, carry):
+                block = edge[s, :, lanes]
+                crossing = jnp.concatenate([block * masks[o, :, lanes] for o in range(3)], axis=0)
+                flux = dot(face_w[:, 0 : 3 * row], crossing)
+                applied = partial[s, :, lanes] + flux[0:row] + flux[row : 2 * row]
+                residual = live[:, lanes] * (load_slab(right_side, s, first, stop) - applied[0:dof])
+                if last:
+                    store_slab(final_residual, s, residual, first)
+                high, low = split(residual)
+                residual_parts[0:dof, lanes] = high
+                residual_parts[row : row + dof, lanes] = high
+                residual_parts[2 * row : 2 * row + dof, lanes] = low
+                rounded = dot(pre_w[...], residual_parts[:, lanes])[0:dof].astype(BF16)
+                source[s, 0:dof, lanes] = rounded
+                state[:, lanes] = inverse[pl.ds(s, 1), lanes] * (
+                    rate_rows[:, lanes] * state[:, lanes] + rounded.astype(F32)
+                )
+                return carry
+
+            lax.fori_loop(0, slabs, finish, 0)
+            offset_out[section, part, 0:dof, :] = state[:, lanes].astype(BF16)
+            offsets.append(offset_copies(section, part))
+            for copy in offsets[part]:
+                copy.start()
         if section == 0:
             for copy in gain_copies:
                 copy.wait()
@@ -234,30 +252,37 @@
             for m in range(1, n_slab):
                 whole = whole * (power * gain_in[m, 0:1, :])
             closing[...] = 1.0 / (1.0 - whole)
-        for copy in offsets:
-            copy.wait()
-        entering = state[...]
-        for m in range(n_slab - 1, 0, -1):
-            entering = offset_in[section, m, 0:dof, :].astype(F32) + (power * gain_in[m, 0:1, :]) * entering
-        state[...] = entering * closing[...]
         field = iterate if section == 0 else smoothed
-
-        def advance(s, carry):
-            value = inverse[pl.ds(s, 1), :] * (rate_rows[...] * state[...] + source[s, 0:dof, :].astype(F32))
-            state[...] = value
-            updated = load_slab(field, s) + RELAX * value.astype(BF16).astype(F32)
-            store_slab(smoothed, s, updated)
-            if not last:
-                high, low = split(updated)
-                cells[s + 1, 0:dof, :] = high
-                cells_low[s + 1, 0:dof, :] = low
-            return carry
-
-        lax.fori_loop(0, slabs, advance, 0)
         if not last:
             field_now = field_copies(section + 1)
-            for copy in field_now:
-                copy.start()
+        for part in range(2):
+            lanes = slice(part * half, (part + 1) * half)
+            first, stop = part * tiles // 2, (part + 1) * tiles // 2
+            for copy in offsets[part]:
+                copy.wait()
+            entering = state[:, lanes]
+            for m in range(n_slab - 1, 0, -1):
+                gain = power * gain_in[m, 0:1, lanes]
+                entering = offset_in[section, part, m, 0:dof, :].astype(F32) + gain * entering
+            state[:, lanes] = entering * closing[:, lanes]
+
+            def advance(s, carry):
+                value = inverse[pl.ds(s, 1), lanes] * (
+                    rate_rows[:, lanes] * state[:, lanes] + source[s, 0:dof, lanes].astype(F32)
+                )
+                state[:, lanes] = value
+                updated = load_slab(field, s, first, stop) + RELAX * value.astype(BF16).astype(F32)
+                store_slab(smoothed, s, updated, first)
+                if not last:
+                    high, low = split(updated)
+                    cells[s + 1, 0:dof, lanes] = high
+                    cells_low[s + 1, 0:dof, lanes] = low
+                return carry
+
+            lax.fori_loop(0, slabs, advance, 0)
+            if not last:
+                for copy in ([field_now[1]] if part == 0 else [field_now[0], field_now[2]]):
+                    copy.start()
 
 
 def on_device(
@@ -272,7 +297,7 @@
     tiles = count // LANES
     vmem = pl.BlockSpec(memory_space=pltpu.VMEM)
     smem = pl.BlockSpec(memory_space=pltpu.SMEM)
-    copies = SECTIONS * (3 + n_slab - 1) + n_slab - 1
+    copies = SECTIONS * (3 + 2 * (n_slab - 1)) + n_slab - 1
 
     def by_dof(value):
         lined = value.transpose(1, 0, 2).reshape(dof, slabs, tiles, LANES)
@@ -295,6 +320,8 @@
             pltpu.VMEM((2, half, half), BF16),
             pltpu.VMEM((faces, slabs, row, count), BF16),
             pltpu.VMEM((faces, slabs, row, count), BF16),
+            pltpu.VMEM((slabs, row, count), F32),
+            pltpu.VMEM((slabs, row, count), BF16),
             pltpu.VMEM((3 * faces, row, count), BF16),
             pltpu.VMEM((row, 3 * faces * row), F32),
             pltpu.VMEM((2 * row, 3 * faces * row), BF16),
@@ -313,8 +340,8 @@
             pltpu.VMEM((SECTIONS, row, count), BF16),
             pltpu.VMEM((8, count), F32),
             pltpu.VMEM((n_slab, 8, count), F32),
-            pltpu.VMEM((SECTIONS, row, count), BF16),
-            pltpu.VMEM((SECTIONS, n_slab, row, count), BF16),
+            pltpu.VMEM((SECTIONS, 2, row, half), BF16),
+            pltpu.VMEM((SECTIONS, 2, n_slab, row, half), BF16),
             pltpu.SemaphoreType.DMA((copies,)),
             pltpu.SemaphoreType.DMA((copies,)),
         ],

time: 55.6 us -> 52.6 us (0.946)
  Pallas kernels: 50.9 us -> 47.9 us
    pallas_call x1, Pallas kernels: 50.9 us -> 47.9 us  [on_device(): pl.pallas_call(functools.partial(smoother, n_sector, n_slab, slabs, dof,...]
where the time goes in v3:
time: 52.6 us; the launch traced here: 52.4 us
  Pallas kernels  47.9 us (91%)
  local copies, waits for them, and re-layouts  3.24 us (6%)
  between operations  1.3 us (2%)
    pallas_call x1, Pallas kernels, on_device(): pl.pallas_call(functools.partial(smoother, n_sector, n_slab, slabs, dof,...  47.9 us
    unnamed x4, local copies, waits for them, and re-layouts  3.24 us

profile of v3, /device:TPU:0, one launch (start us, length us, event | category | flops | bytes accessed | tf_op | source)
XLA Modules:
  0.0 52.4 jit_solution(12673965954041812230)
XLA Ops:
  1.3 47.9 %shard_map.140 = (f32[1920,128]{1,0:T(8,128)}, f32[1920,128]{1,0:T(8,128)}) custom-call(f32[1920,128]{1,0:T(8,128)} %bitcast.31, f32[1920,128]{1,0:T(8,128)} %bitcast.32, f32[3,8,512]{2,1,0:T(8,128)} %bitcast.36, f32[8,512]{1,0:T(8,128)} %scale.1, f32[1,60]{1,0:T(1,128)} %bitcast.37, s32[5,512]{1,0:T(8,128)} %index.1, s32[5,512]{1,0:T(8,128)} %side.1, ...), custom_call_target="tpu_custom_call" | custom-call | tf_op jit(solution)/shard_map/pallas_call | solution.py:311
  49.2 0.0 copy-start
  49.2 2.3 %copy.18 = f32[8,60,512]{2,0,1:T(8,128)} copy(f32[8,60,512]{2,0,1:T(8,128)} %bitcast.34) | data formatting | bytes 1966080
  51.5 0.0 copy-done
  51.5 0.9 %copy.19 = f32[8,60,512]{2,0,1:T(8,128)} copy(f32[8,60,512]{2,0,1:T(8,128)S(1)} %bitcast.33) | data formatting | bytes 1966080
Async XLA Ops:
  49.2 2.3 %copy-start = (f32[1920,128]{1,0:T(8,128)S(1)}, f32[1920,128]{1,0:T(8,128)}, u32[]{:S(2)}) copy-start(f32[1920,128]{1,0:T(8,128)} %get-tuple-element.5) | copy-start | bytes 2949124

commit v4 on v3

--- a/solution.py
+++ b/solution.py
@@ -204,7 +204,7 @@
             partial[s] = applied + flux[0:row] + flux[row : 2 * row] + flux_low
             return carry
 
-        lax.fori_loop(0, slabs, apply, 0)
+        lax.fori_loop(0, slabs, apply, 0, unroll=min(2, slabs))
         for copy in field_now:
             copy.wait()
         slab_before = previous[section]
@@ -230,17 +230,20 @@
                 if last:
                     store_slab(final_residual, s, residual, first)
                 high, low = split(residual)
-                residual_parts[0:dof, lanes] = high
-                residual_parts[row : row + dof, lanes] = high
-                residual_parts[2 * row : 2 * row + dof, lanes] = low
-                rounded = dot(pre_w[...], residual_parts[:, lanes])[0:dof].astype(BF16)
-                source[s, 0:dof, lanes] = rounded
+                residual_parts[s, 0:dof, lanes] = high
+                residual_parts[s, row : row + dof, lanes] = high
+                residual_parts[s, 2 * row : 2 * row + dof, lanes] = low
+                source[s, 0:dof, lanes] = dot(pre_w[...], residual_parts[s, :, lanes])[0:dof].astype(BF16)
+                return carry
+
+            def collect(s, carry):
                 state[:, lanes] = inverse[pl.ds(s, 1), lanes] * (
-                    rate_rows[:, lanes] * state[:, lanes] + rounded.astype(F32)
+                    rate_rows[:, lanes] * state[:, lanes] + source[s, 0:dof, lanes].astype(F32)
                 )
                 return carry
 
-            lax.fori_loop(0, slabs, finish, 0)
+            lax.fori_loop(0, slabs, finish, 0, unroll=min(4, slabs))
+            lax.fori_loop(0, slabs, collect, 0, unroll=min(2, slabs))
             offset_out[section, part, 0:dof, :] = state[:, lanes].astype(BF16)
             offsets.append(offset_copies(section, part))
             for copy in offsets[part]:
@@ -279,7 +282,7 @@
                     cells_low[s + 1, 0:dof, lanes] = low
                 return carry
 
-            lax.fori_loop(0, slabs, advance, 0)
+            lax.fori_loop(0, slabs, advance, 0, unroll=min(2, slabs))
             if not last:
                 for copy in ([field_now[1]] if part == 0 else [field_now[0], field_now[2]]):
                     copy.start()
@@ -329,7 +332,7 @@
             pltpu.VMEM((4 * row, 6 * row), BF16),
             pltpu.VMEM((row, 3 * row), F32),
             pltpu.VMEM((row, 3 * row), BF16),
-            pltpu.VMEM((3 * row, count), BF16),
+            pltpu.VMEM((slabs, 3 * row, count), BF16),
             pltpu.VMEM((slabs, row, count), BF16),
             pltpu.VMEM((slabs, count), F32),
             pltpu.VMEM((dof, count), F32),

time: 52.6 us -> 49.9 us (0.949)
  Pallas kernels: 47.9 us -> 45.2 us
    pallas_call x1, Pallas kernels: 47.9 us -> 45.2 us  [on_device(): pl.pallas_call(functools.partial(smoother, n_sector, n_slab, slabs, dof,...]
where the time goes in v4:
time: 49.9 us; the launch traced here: 49.8 us
  Pallas kernels  45.2 us (91%)
  local copies, waits for them, and re-layouts  3.24 us (6%)
  between operations  1.3 us (3%)
    pallas_call x1, Pallas kernels, on_device(): pl.pallas_call(functools.partial(smoother, n_sector, n_slab, slabs, dof,...  45.2 us
    unnamed x4, local copies, waits for them, and re-layouts  3.24 us

profile of v4, /device:TPU:0, one launch (start us, length us, event | category | flops | bytes accessed | tf_op | source)
XLA Modules:
  0.0 49.8 jit_solution(12342250987251589137)
XLA Ops:
  1.3 45.2 %shard_map.140 = (f32[1920,128]{1,0:T(8,128)}, f32[1920,128]{1,0:T(8,128)}) custom-call(f32[1920,128]{1,0:T(8,128)} %bitcast.31, f32[1920,128]{1,0:T(8,128)} %bitcast.32, f32[3,8,512]{2,1,0:T(8,128)} %bitcast.36, f32[8,512]{1,0:T(8,128)} %scale.1, f32[1,60]{1,0:T(1,128)} %bitcast.37, s32[5,512]{1,0:T(8,128)} %index.1, s32[5,512]{1,0:T(8,128)} %side.1, ...), custom_call_target="tpu_custom_call" | custom-call | tf_op jit(solution)/shard_map/pallas_call | solution.py:314
  46.5 0.0 copy-start
  46.5 2.3 %copy.18 = f32[8,60,512]{2,0,1:T(8,128)} copy(f32[8,60,512]{2,0,1:T(8,128)} %bitcast.34) | data formatting | bytes 1966080
  48.8 0.0 copy-done
  48.8 0.9 %copy.19 = f32[8,60,512]{2,0,1:T(8,128)} copy(f32[8,60,512]{2,0,1:T(8,128)S(1)} %bitcast.33) | data formatting | bytes 1966080
Async XLA Ops:
  46.5 2.3 %copy-start = (f32[1920,128]{1,0:T(8,128)S(1)}, f32[1920,128]{1,0:T(8,128)}, u32[]{:S(2)}) copy-start(f32[1920,128]{1,0:T(8,128)} %get-tuple-element.5) | copy-start | bytes 2949124
